TPU v7x, 32 devices: a whole 2x2x4 slice. The times are simulated.
32 devices in a mesh: wide: 8 (over z, x), narrow: 4 (over y, core).
Axes of the slice: x: 2, y: 2, z: 4, core: 2. Of those that a mesh axis runs over, the one named last changes fastest.
Arguments:
- tile_data: bfloat16 [10240, 128, 128], P(('wide', 'narrow')), may hold values from -0.119628906 to 0.119628906
- tile_user: int32 [10240], P(('wide', 'narrow')), may hold values from 0 to 15
- tile_item: int32 [10240], P(('wide', 'narrow')), may hold values from 0 to 7
- tile_word: int32 [10240], P(('wide', 'narrow')), may hold values from 0 to 4095
- tile_month: int32 [10240], P(('wide', 'narrow')), may hold values from 0 to 999
- tile_live: int32 [32], P(('wide', 'narrow')), may hold values from 160 to 320, as said below
- user_need: int32 [32, 16], P(('wide', 'narrow')), may hold values from 0 to 127, as said below
- item_need: int32 [32, 8], P(('wide', 'narrow')), may hold values from 0 to 127, as said below
- user_slot: int32 [128], replicated, may hold values from 0 to 127, as said below
- item_slot: int32 [128], replicated, may hold values from 0 to 127, as said below
- user_factor: bfloat16 [16384, 128], P('wide'), may hold values from -6 to 6
- word_factor: bfloat16 [4096, 128], replicated, may hold values from -6 to 6
- month_factor: bfloat16 [1000, 128], replicated, may hold values from -6 to 6
Outputs:
- item_rows: float32 [16384, 128], P(('wide', 'narrow'))
Inputs may be any that keep to these rules, and one draw needn't show every extreme that they name: user_slot is a permutation; the owner of user block b is user_slot[b] // 16. item_slot is a permutation; the owner of item block b is item_slot[b] // 16. `user_need`: entries k * 2 to k * 2 + 1 of each row are distinct user blocks whose owner is k. `item_need`: entry k of each row is an item block whose owner is k. `tile_live`: some device has all its slots live.
All inputs are finite; a program needn't handle non-finite values.
Results may differ from a plain program's by a relative error of at most 0.0029.
Values may be sent and summed in bfloat16 or wider, within the bound.
No kernel may reach another device: no remote copies, remote signals or barrier semaphores. Data moves between devices by JAX's collectives and lax.ppermute only.
A program may use at most 128 MiB of HBM per device.

v0:
```python
import jax
import jax.numpy as jnp
from jax import lax
from jax.sharding import PartitionSpec as P


def shards(
    tile_data,
    tile_user,
    tile_item,
    tile_word,
    tile_month,
    tile_live,
    user_need,
    item_need,
    user_slot,
    item_slot,
    user_factor,
    word_factor,
    month_factor,
):
    wide_count = lax.axis_size("wide")
    tile_count = tile_data.shape[0]
    block_side = tile_data.shape[1]
    rank_width = user_factor.shape[1]
    owned_users = user_factor.shape[0] // block_side
    items_owned = item_slot.shape[0] // wide_count
    touched = item_need.shape[1]
    item_local = (item_slot[item_need[0]] % items_owned).reshape(wide_count, -1)
    item_from = lax.all_to_all(item_local, "wide", split_axis=0, concat_axis=0, tiled=True)
    user_place = user_slot[user_need[0]]
    wanted = (user_place % owned_users).reshape(wide_count, -1)
    asked_for = lax.all_to_all(wanted, "wide", split_axis=0, concat_axis=0, tiled=True)
    answer = user_factor.reshape(owned_users, block_side, rank_width)[asked_for]
    fetched = lax.all_to_all(answer, "wide", split_axis=0, concat_axis=0, tiled=True).reshape(
        -1, block_side, rank_width
    )
    word_month = word_factor[tile_word].astype(jnp.float32) * month_factor[tile_month].astype(
        jnp.float32
    )
    scaled = (fetched[tile_user].astype(jnp.float32) * word_month[:, None, :]).astype(jnp.bfloat16)
    contrib = jnp.einsum("tab,tar->tbr", tile_data, scaled, preferred_element_type=jnp.float32)
    is_live = lax.iota(jnp.int32, tile_count) < tile_live[0]
    group_ids = jnp.where(is_live, tile_item, touched)
    partial_value = jax.ops.segment_sum(contrib, group_ids, num_segments=touched + 1)[:touched]
    arrived = lax.all_to_all(
        partial_value.reshape(wide_count, -1, block_side, rank_width),
        "wide",
        split_axis=0,
        concat_axis=0,
        tiled=True,
    )
    arrived = arrived.reshape(-1, block_side, rank_width)
    slot_ids = item_from.reshape(-1)
    placing = (slot_ids[:, None] == lax.iota(jnp.int32, items_owned)[None, :]).astype(jnp.float32)
    owner_sum = jnp.einsum("kj,kbr->jbr", placing, arrived, precision=lax.Precision.HIGHEST)
    owned_rows = lax.psum_scatter(owner_sum, "narrow", scatter_dimension=0, tiled=True)
    return owned_rows.reshape(-1, rank_width)


def solution(mesh):
    return jax.shard_map(
        shards,
        mesh=mesh,
        in_specs=(
            P(("wide", "narrow"), None, None),
            P(("wide", "narrow")),
            P(("wide", "narrow")),
            P(("wide", "narrow")),
            P(("wide", "narrow")),
            P(("wide", "narrow")),
            P(("wide", "narrow"), None),
            P(("wide", "narrow"), None),
            P(),
            P(),
            P("wide", None),
            P(),
            P(),
        ),
        out_specs=P(("wide", "narrow"), None),
        check_vma=False,
    )
```

profile of v0, /device:TPU:0, one launch (start us, length us, event | category | flops | bytes accessed | tf_op | source)
XLA Modules:
  0.0 186.1 jit_solution(14022994367051493420)
XLA Ops:
  6.5 0.0 copy-start
  6.5 0.7 fusion.13
  7.3 1.3 gather_fusion.1
  8.6 0.1 gather.25
  8.7 0.6 add_select_fusion
  9.3 7.3 %all-to-all-start.1 = ((s32[8,1,2]{2,1,0:T(1,128)}), s32[8,1,2]{2,1,0:T(1,128)S(1)}, u32[]{:S(2)}, u32[]{:S(2)}) async-start(s32[8,1,2]{2,1,0:T(1,128)} %bitcast.8), calls=%async_computation.1 | async-start | bytes 8192 | tf_op jit(solution)/shard_map/all_to_all | solution.py:33
  16.6 0.7 compare_select_fusion.1
  17.3 0.7 compare_select_fusion
  18.0 0.7 fusion.12
  18.6 1.3 gather_fusion
  19.9 3.1 %all-to-all-done.1 = s32[8,1,2]{2,1,0:T(1,128)S(1)} async-done(((s32[8,1,2]{2,1,0:T(1,128)}), s32[8,1,2]{2,1,0:T(1,128)S(1)}, u32[]{:S(2)}, u32[]{:S(2)}) %all-to-all-start.1) | async-done | bytes 96 | tf_op jit(solution)/shard_map/all_to_all | solution.py:33
  23.0 0.1 copy.35
  23.1 0.1 copy.36
  23.2 0.1 reshape.227
  23.3 2.5 %gather_fusion.2 = bf16[16,128,128]{2,1,0:T(8,128)(2,1)} fusion(bf16[16,128,128]{2,1,0:T(8,128)(2,1)} %bitcast.35, s32[1024]{0:T(1024)S(1)} %pad_clamp_fusion.3), kind=kCustom, calls=%fused_computation.2 | custom fusion | bytes 1048640 | tf_op jit(solution)/shard_map/gather | solution.py:34
  25.7 3.5 %all-to-all-start.2 = ((bf16[8,2,128,128]{3,2,1,0:T(8,128)(2,1)}), bf16[8,2,128,128]{3,2,1,0:T(8,128)(2,1)S(1)}, u32[]{:S(2)}, u32[]{:S(2)}) async-start(bf16[8,2,128,128]{3,2,1,0:T(8,128)(2,1)} %bitcast.10), calls=%async_computation.2 | async-start | bytes 1048576 | tf_op jit(solution)/shard_map/all_to_all | solution.py:35
  29.9 0.7 copy.33
  30.6 0.0 copy-done
  30.6 1.4 gather_fusion.4
  32.0 2.1 %gather_fusion.5 = bf16[320,128]{1,0:T(8,128)(2,1)S(1)} fusion(bf16[1000,128]{1,0:T(8,128)(2,1)} %param.25, s32[1024]{0:T(1024)S(1)} %pad_clamp_fusion), kind=kCustom, calls=%fused_computation.5 | custom fusion | bytes 165120 | tf_op jit(solution)/shard_map/gather | solution.py:38
  34.1 0.7 compare_select_fusion.2
  34.8 0.7 fusion.10
  35.5 7.1 %all-to-all-done.2 = bf16[8,2,128,128]{3,2,1,0:T(8,128)(2,1)S(1)} async-done(((bf16[8,2,128,128]{3,2,1,0:T(8,128)(2,1)}), bf16[8,2,128,128]{3,2,1,0:T(8,128)(2,1)S(1)}, u32[]{:S(2)}, u32[]{:S(2)}) %all-to-all-start.2) | async-done | bytes 524320 | tf_op jit(solution)/shard_map/all_to_all | solution.py:35
  42.6 3.7 %all-to-all-start = ((s32[8,1,1]{2,1,0:T(1,128)}), s32[8,1,1]{2,1,0:T(1,128)S(1)}, u32[]{:S(2)}, u32[]{:S(2)}) async-start(s32[8,1,1]{2,1,0:T(1,128)} %copy.33), calls=%async_computation | async-start | bytes 8192 | tf_op jit(solution)/shard_map/all_to_all | solution.py:30
  46.3 10.7 %gather_fusion.3 = bf16[320,128,128]{2,1,0:T(8,128)(2,1)} fusion(bf16[16,128,128]{2,1,0:T(8,128)(2,1)S(1)} %bitcast.34, s32[1024]{0:T(1024)S(1)} %pad_clamp_fusion.2), kind=kCustom, calls=%fused_computation.3 | custom fusion | bytes 20972800 | tf_op jit(solution)/shard_map/gather | solution.py:41
  57.0 12.9 %fusion.2 = f32[320,128,128]{1,2,0:T(8,128)} fusion(bf16[320,128,128]{2,1,0:T(8,128)(2,1)} %param.13, bf16[320,128,128]{2,1,0:T(8,128)(2,1)} %gather_fusion.3, f32[320,128]{1,0:T(8,128)S(1)} %convert_multiply_fusion), kind=kOutput, calls=%fused_computation.10 | convolution fusion | flops 1357905920 | bytes 42106880 | tf_op jit(solution)/shard_map/tab,tar->tbr/dot_general | solution.py:42
  69.9 21.1 %copy.38 = f32[320,128,128]{2,1,0:T(8,128)} copy(f32[320,128,128]{1,2,0:T(8,128)} %fusion.2) | data formatting | bytes 41943040 | tf_op jit(solution)/shard_map/tab,tar->tbr/dot_general | solution.py:42
  91.1 0.0 copy-start.1
  91.1 41.9 %scatter_fusion = f32[9,128,128]{2,1,0:T(8,128)S(1)} fusion(f32[9,128,128]{2,1,0:T(8,128)S(1)} %broadcast_in_dim.24, s32[320]{0:T(512)S(1)} %fusion.10, f32[320,128,128]{2,1,0:T(8,128)} %copy.38), kind=kCustom, calls=%fused_computation.6 | custom fusion | flops 5242880 | bytes 62915840 | tf_op jit(solution)/shard_map/scatter-add | solution.py:45
  133.0 0.8 slice_bitcast_fusion
  133.8 0.0 all-to-all-done
  133.8 6.0 %all-to-all-start.3 = ((f32[8,1,128,128]{3,2,1,0:T(8,128)}), f32[8,1,128,128]{3,2,1,0:T(8,128)S(1)}, u32[]{:S(2)}, u32[]{:S(2)}) async-start(f32[8,1,128,128]{3,2,1,0:T(8,128)} %slice_bitcast_fusion), calls=%async_computation.3 | async-start | bytes 1048576 | tf_op jit(solution)/shard_map/all_to_all | solution.py:46
  139.8 0.0 reduce-scatter.2.cloned.1.call-start
  139.8 0.2 reduce
  140.0 12.9 %all-to-all-done.3 = f32[8,1,128,128]{3,2,1,0:T(8,128)S(1)} async-done(((f32[8,1,128,128]{3,2,1,0:T(8,128)}), f32[8,1,128,128]{3,2,1,0:T(8,128)S(1)}, u32[]{:S(2)}, u32[]{:S(2)}) %all-to-all-start.3) | async-done | bytes 524320 | tf_op jit(solution)/shard_map/all_to_all | solution.py:46
  153.0 0.9 fusion.3
  153.8 1.3 copy.41
  155.1 0.0 reduce-scatter.2.cloned.1.call-update
  155.1 24.1 %reduce-scatter.2.cloned.1.call-done = f32[4,128,128]{2,1,0:T(8,128)} async-done(((f32[16,128,128]{2,1,0:T(8,128)}), f32[4,128,128]{2,1,0:T(8,128)}) %reduce-scatter.2.cloned.1.call-update) | async-done | bytes 262160 | tf_op jit(solution)/shard_map/reduce_scatter | solution.py:57
  179.2 0.0 copy-done.1
  (10 shorter events, 0.1 us)
Async XLA Ops:
  6.5 24.0 %copy-start = (bf16[4096,128]{1,0:T(8,128)(2,1)S(1)}, bf16[4096,128]{1,0:T(8,128)(2,1)}, u32[]{:S(2)}) copy-start(bf16[4096,128]{1,0:T(8,128)(2,1)} %param.24) | copy-start | bytes 3145732
  9.3 13.7 %all-to-all-start.1 = ((s32[8,1,2]{2,1,0:T(1,128)}), s32[8,1,2]{2,1,0:T(1,128)S(1)}, u32[]{:S(2)}, u32[]{:S(2)}) async-start(s32[8,1,2]{2,1,0:T(1,128)} %bitcast.8), calls=%async_computation.1 | async-start | bytes 8192 | tf_op jit(solution)/shard_map/all_to_all | solution.py:33
  25.7 16.9 %all-to-all-start.2 = ((bf16[8,2,128,128]{3,2,1,0:T(8,128)(2,1)}), bf16[8,2,128,128]{3,2,1,0:T(8,128)(2,1)S(1)}, u32[]{:S(2)}, u32[]{:S(2)}) async-start(bf16[8,2,128,128]{3,2,1,0:T(8,128)(2,1)} %bitcast.10), calls=%async_computation.2 | async-start | bytes 1048576 | tf_op jit(solution)/shard_map/all_to_all | solution.py:35
  42.6 91.2 %all-to-all-start = ((s32[8,1,1]{2,1,0:T(1,128)}), s32[8,1,1]{2,1,0:T(1,128)S(1)}, u32[]{:S(2)}, u32[]{:S(2)}) async-start(s32[8,1,1]{2,1,0:T(1,128)} %copy.33), calls=%async_computation | async-start | bytes 8192 | tf_op jit(solution)/shard_map/all_to_all | solution.py:30
  91.1 88.1 %copy-start.1 = (bf16[4096,128]{1,0:T(8,128)(2,1)S(1)}, bf16[4096,128]{1,0:T(8,128)(2,1)}, u32[]{:S(2)}) copy-start(bf16[4096,128]{1,0:T(8,128)(2,1)} %param.24) | copy-start | bytes 3145732
  133.8 19.2 %all-to-all-start.3 = ((f32[8,1,128,128]{3,2,1,0:T(8,128)}), f32[8,1,128,128]{3,2,1,0:T(8,128)S(1)}, u32[]{:S(2)}, u32[]{:S(2)}) async-start(f32[8,1,128,128]{3,2,1,0:T(8,128)} %slice_bitcast_fusion), calls=%async_computation.3 | async-start | bytes 1048576 | tf_op jit(solution)/shard_map/all_to_all | solution.py:46
  139.8 39.5 %reduce-scatter.2.cloned.1.call-start = ((), (), s32[]{:S(2)}) async-start(), calls=%async_computation.5 | async-start | bytes 1310720 | tf_op jit(solution)/shard_map/reduce_scatter | solution.py:57
Sparse Core Ops, SparseCore 0:
  155.3 23.9 reduce-scatter.1
where the time goes:
time: 188 us; the launch traced here: 186 us
  waiting for transfers between devices  47.2 us (25%)
  other arithmetic  46.9 us (25%)
  local copies, waits for them, and re-layouts  43.6 us (23%)
  starting transfers between devices  20.5 us (11%)
  between operations  14.1 us (8%)
  matrix products  13.8 us (7%)
    scatter-add x1, other arithmetic, shards(): jax.ops.segment_sum(contrib, group_ids, num_segments=touched + 1)[:touched]  41.9 us
    reduce_scatter x1, waiting for transfers between devices, shards(): lax.psum_scatter(owner_sum, 'narrow', scatter_dimension=0, tiled=True)  24.1 us
    dot_general x1, local copies, waits for them, and re-layouts, shards(): jnp.einsum('tab,tar->tbr', tile_data, scaled, preferred_element_type=jnp....  21.1 us
    dot_general x1, matrix products, shards(): jnp.einsum('tab,tar->tbr', tile_data, scaled, preferred_element_type=jnp....  12.9 us
    all_to_all x1, waiting for transfers between devices, shards(): lax.all_to_all(partial_value.reshape(wide_count, -1, block_side, rank_wid...  12.9 us
    gather x1, local copies, waits for them, and re-layouts, shards(): fetched[tile_user].astype(jnp.float32) * word_month[:, None, :]  10.7 us
    all_to_all x1, starting transfers between devices, shards(): lax.all_to_all(wanted, 'wide', split_axis=0, concat_axis=0, tiled=True)  7.28 us
    all_to_all x1, waiting for transfers between devices, shards(): lax.all_to_all(answer, 'wide', split_axis=0, concat_axis=0, tiled=True)  7.08 us
  transfers between devices with their start and end apart: 5, of which 4 were waited for; matrix products, arithmetic and copies ran while one was open for 52% of the time, Pallas kernels for 0%

commit v1 on v0

v1 whole, which is shorter than its diff:
```python
import functools

import jax
import jax.numpy as jnp
from jax import lax
from jax.experimental import pallas as pl
from jax.experimental.pallas import tpu as pltpu
from jax.sharding import PartitionSpec as P

CONTRACT_MIB = 12
ANSWER_MIB = 12
RANK_MIB = 63
TURN_MIB = 12
TURN = 32
GROUP = 4
CHUNKS = 12
SMEM = pl.BlockSpec(memory_space=pltpu.SMEM)
VMEM = pl.BlockSpec(memory_space=pltpu.VMEM)
HBM = pl.BlockSpec(memory_space=pltpu.HBM)


def rank_kernel(
    per, pad_count, me, live, user, word, month, item, words, months,
    plan, scale,
    word_held, month_held, word_rows, month_rows, place_v, count_v, offset_v,
    place, count, offset, fetch,
):
    tile_count = item.shape[0]
    touched = count.shape[1]
    slots = scale.shape[0]
    dump = slots - 16
    tables = [
        pltpu.make_async_copy(words, word_held, fetch.at[3]),
        pltpu.make_async_copy(months, month_held, fetch.at[4]),
    ]
    for copy in tables:
        copy.start()
    rows = lax.broadcasted_iota(jnp.int32, (touched, tile_count), 0)
    lanes = lax.broadcasted_iota(jnp.int32, (touched, tile_count), 1)
    one = jnp.where((rows == item[...].reshape(1, tile_count)) & (lanes < live[0]), 1.0, 0.0)
    one_half = one.astype(jnp.bfloat16)
    before = jnp.where(
        lax.broadcasted_iota(jnp.int32, (tile_count, tile_count), 0)
        < lax.broadcasted_iota(jnp.int32, (tile_count, tile_count), 1),
        1.0,
        0.0,
    ).astype(jnp.bfloat16)
    rank = jnp.dot(one_half, before, preferred_element_type=jnp.float32)
    small_rows = lax.broadcasted_iota(jnp.int32, (touched, touched), 0)
    small_lanes = lax.broadcasted_iota(jnp.int32, (touched, touched), 1)
    chunks_of = lambda n: jnp.floor((n + (GROUP - 1)) * (1.0 / GROUP))
    count_column = jnp.sum(one, axis=1, keepdims=True)
    chunks_column = jnp.broadcast_to(chunks_of(count_column), (touched, 128)).astype(jnp.bfloat16)
    offset_column = GROUP * jnp.dot(
        jnp.where(small_lanes < small_rows, 1.0, 0.0).astype(jnp.bfloat16),
        chunks_column,
        preferred_element_type=jnp.float32,
    )[:, :1]
    here = jnp.sum(one * (rank + offset_column), axis=0, keepdims=True)
    lane = lax.broadcasted_iota(jnp.int32, (1, tile_count), 1)
    place_v[...] = jnp.where(lane < live[0], here.astype(jnp.int32), dump + lax.rem(lane, 16))
    count_row = lax.dot_general(
        jnp.ones((8, tile_count), jnp.bfloat16),
        one_half,
        (((1,), (1,)), ((), ())),
        preferred_element_type=jnp.float32,
    )
    offset_row = GROUP * jnp.dot(
        chunks_of(count_row).astype(jnp.bfloat16),
        jnp.where(small_rows < small_lanes, 1.0, 0.0).astype(jnp.bfloat16),
        preferred_element_type=jnp.float32,
    )
    count_v[...] = count_row.astype(jnp.int32)
    offset_v[...] = offset_row.astype(jnp.int32)
    fetched = [
        pltpu.make_async_copy(source, sink, fetch.at[n])
        for n, (source, sink) in enumerate(((place_v, place), (count_v, count), (offset_v, offset)))
    ]
    for copy in fetched:
        copy.start()
    for copy in tables:
        copy.wait()
    word_rows[...] = word_held[...].astype(jnp.float32)
    month_rows[...] = month_held[...].astype(jnp.float32)
    for copy in fetched:
        copy.wait()
    places = slots + slots // GROUP + 1
    pads = places + tile_count
    for n in range(pad_count):
        plan[pads + n] = dump + n % 16
    nothing = jnp.zeros((1, scale.shape[1]), scale.dtype)

    def blank(n, p):
        plan[pads + n] = p
        plan[p] = 0
        scale[pl.ds(p, 1), :] = nothing

    def pad(q, blanks):
        first, n = offset[0, q], count[0, q]
        chunks = (n + GROUP - 1) // GROUP

        def mark(c, _):
            plan[slots + first // GROUP + c] = q
            return 0

        def fill(p, blanks):
            blank(blanks, p)
            return blanks + 1

        lax.fori_loop(0, chunks, mark, 0)
        return lax.fori_loop(first + n, first + chunks * GROUP, fill, blanks)

    blanks = lax.fori_loop(0, touched, pad, 0)
    last = offset[0, touched - 1] // GROUP
    chunks = last + (count[0, touched - 1] + GROUP - 1) // GROUP
    for c in range(CHUNKS - 1):
        plan[slots + chunks + c] = 0
        for g in range(GROUP):
            blank(blanks + c * GROUP + g, (chunks + c) * GROUP + g)
    plan[places - 1] = (chunks + CHUNKS - 1) // CHUNKS

    def put(c, _):
        for n in range(16):
            t = c * 16 + n
            p = place[0, t]
            scale[pl.ds(p, 1), :] = (
                word_rows[pl.ds(word[t], 1), :] * month_rows[pl.ds(month[t], 1), :]
            )
            u = user[t]
            plan[p] = (lax.div(u, per) ^ me[0]) * per + lax.rem(u, per)
            plan[places + t] = p
        return 0

    lax.fori_loop(0, tile_count // 16, put, 0)


def slots_for(tile_count, touched):
    per_step = GROUP * CHUNKS
    return -(-(tile_count + touched * (GROUP - 1)) // per_step) * per_step + per_step + 16


def rank(me, per, live, user, item, word, month, words, months, touched):
    tile_count = user.shape[0]
    width = words.shape[1]
    slots = slots_for(tile_count, touched)
    pads = touched * (GROUP - 1) + (CHUNKS - 1) * GROUP
    shape = jax.ShapeDtypeStruct
    return pl.pallas_call(
        functools.partial(rank_kernel, per, pads),
        out_shape=(
            shape((slots + slots // GROUP + 1 + tile_count + pads,), jnp.int32),
            shape((slots, width), jnp.float32),
        ),
        in_specs=[SMEM] * 5 + [VMEM, HBM, HBM],
        out_specs=(SMEM, VMEM),
        scratch_shapes=[
            pltpu.VMEM(words.shape, words.dtype),
            pltpu.VMEM(months.shape, months.dtype),
            pltpu.VMEM(words.shape, jnp.float32),
            pltpu.VMEM(months.shape, jnp.float32),
            pltpu.VMEM((1, tile_count), jnp.int32),
            pltpu.VMEM((8, touched), jnp.int32),
            pltpu.VMEM((8, touched), jnp.int32),
            pltpu.SMEM((1, tile_count), jnp.int32),
            pltpu.SMEM((8, touched), jnp.int32),
            pltpu.SMEM((8, touched), jnp.int32),
            pltpu.SemaphoreType.DMA((5,)),
        ],
        compiler_params=pltpu.CompilerParams(vmem_limit_bytes=RANK_MIB << 20),
        cost_estimate=pl.CostEstimate(flops=1 << 33, bytes_accessed=1 << 25, transcendentals=0),
        name="rank",
    )(me, live, user, word, month, item, words, months)


def turn_kernel(pad_count, plan, tiles, turned):
    tile_count = tiles.shape[0]
    slots = turned.shape[0]
    places = slots + slots // GROUP + 1
    nothing = jnp.zeros(turned.shape[1:], turned.dtype)

    def clear(n, _):
        turned[plan[places + tile_count + n]] = nothing
        return 0

    lax.fori_loop(0, pad_count, clear, 0, unroll=4)

    def put(c, _):
        for n in range(TURN):
            t = c * TURN + n
            turned[plan[places + t]] = tiles[t].T
        return 0

    lax.fori_loop(0, tile_count // TURN, put, 0)


def turn(plan, tiles, slots):
    tile_count, side = tiles.shape[:2]
    pads = plan.shape[0] - (slots + slots // GROUP + 1 + tile_count)
    return pl.pallas_call(
        functools.partial(turn_kernel, pads),
        out_shape=jax.ShapeDtypeStruct((slots, side, side), tiles.dtype),
        in_specs=[SMEM, VMEM],
        out_specs=VMEM,
        compiler_params=pltpu.CompilerParams(vmem_limit_bytes=TURN_MIB << 20),
        cost_estimate=pl.CostEstimate(
            flops=1 << 30, bytes_accessed=4 * tiles.size, transcendentals=0
        ),
        name="turn",
    )(plan, tiles)


def ask_kernel(user_need, item_need, need):
    wide = need.shape[0]
    per_user, per_item = user_need.shape[1] // wide, item_need.shape[1] // wide
    for k in range(wide):
        for j in range(per_user):
            need[k, 0, j] = user_need[0, k * per_user + j]
        for j in range(per_item):
            need[k, 0, per_user + j] = item_need[0, k * per_item + j]


def ask(user_need, item_need, wide):
    per = (user_need.shape[1] + item_need.shape[1]) // wide
    return pl.pallas_call(
        ask_kernel,
        out_shape=jax.ShapeDtypeStruct((wide, 1, per), jnp.int32),
        in_specs=[SMEM, SMEM],
        out_specs=SMEM,
        compiler_params=pltpu.CompilerParams(vmem_limit_bytes=63 << 20),
        name="ask",
    )(user_need, item_need)


def answer_kernel(owned, per, me, heard, slot, blocks, *outs):
    for d, out in enumerate(outs):
        k = me[0] ^ d
        for j in range(per):
            out[j] = blocks[lax.rem(slot[heard[k, 0, j]], owned)]


def answer(me, heard, slot, blocks, per):
    owned, side, width = blocks.shape
    wide = heard.shape[0]
    return pl.pallas_call(
        functools.partial(answer_kernel, owned, per),
        out_shape=(jax.ShapeDtypeStruct((per, side, width), blocks.dtype),) * wide,
        in_specs=[SMEM, SMEM, SMEM, VMEM],
        out_specs=(VMEM,) * wide,
        compiler_params=pltpu.CompilerParams(vmem_limit_bytes=ANSWER_MIB << 20),
        cost_estimate=pl.CostEstimate(flops=1 << 33, bytes_accessed=1 << 25, transcendentals=0),
        name="answer",
    )(me, heard, slot, blocks)


def contract_kernel(plan, scale, turned, *refs):
    fetched, (out, wide_blocks, total) = refs[:-3], refs[-3:]
    per = fetched[0].shape[0]
    slots = scale.shape[0]
    per_step = GROUP * CHUNKS
    for d, blocks in enumerate(fetched):
        for j in range(per):
            wide_blocks[d * per + j] = blocks[j].astype(jnp.float32)
    total[...] = jnp.zeros_like(total)

    def step(i, _):
        first = i * per_step
        for c in range(CHUNKS):
            left, right = [], []
            for g in range(GROUP):
                p = first + c * GROUP + g
                left.append(turned[p])
                right.append((wide_blocks[plan[p]] * scale[pl.ds(p, 1), :]).astype(jnp.bfloat16))
            part = jnp.dot(
                jnp.concatenate(left, 1),
                jnp.concatenate(right, 0),
                preferred_element_type=jnp.float32,
            )
            q = plan[slots + i * CHUNKS + c]
            total[q] = total[q] + part
        return 0

    lax.fori_loop(0, plan[slots + slots // GROUP], step, 0)
    out[...] = total[...].astype(out.dtype)


def contract(plan, scale, turned, fetched, touched):
    per, side, width = fetched[0].shape
    return pl.pallas_call(
        contract_kernel,
        out_shape=jax.ShapeDtypeStruct((touched, side, width), jnp.bfloat16),
        in_specs=[SMEM, VMEM, VMEM] + [VMEM] * len(fetched),
        out_specs=VMEM,
        scratch_shapes=[
            pltpu.VMEM((len(fetched) * per, side, width), jnp.float32),
            pltpu.VMEM((touched, side, width), jnp.float32),
        ],
        compiler_params=pltpu.CompilerParams(vmem_limit_bytes=CONTRACT_MIB << 20),
        cost_estimate=pl.CostEstimate(
            flops=2 * turned.size * width, bytes_accessed=turned.size, transcendentals=0
        ),
        name="contract",
    )(plan, scale, turned, *fetched)


def merge_kernel(items_owned, per, me, heard, slot, parts, mine, *rest):
    sends, total = rest[:-1], rest[-1]
    share = mine.shape[0]
    total[...] = jnp.zeros_like(total)

    base = heard.shape[2] - per

    def add(k, _):
        for n in range(per):
            j = lax.rem(slot[heard[k, 0, base + n]], items_owned)
            total[j] = total[j] + parts[k * per + n].astype(jnp.float32)
        return 0

    lax.fori_loop(0, heard.shape[0], add, 0)
    for d in range(items_owned // share):
        first = (me[0] ^ d) * share
        for j in range(share):
            if d == 0:
                mine[j] = total[first + j]
            else:
                sends[d - 1][j] = total[first + j].astype(jnp.bfloat16)


def merge(me, heard, slot, parts, items_owned, members, per):
    side, width = parts.shape[1:]
    share = items_owned // members
    piece = lambda kind: jax.ShapeDtypeStruct((share, side, width), kind)
    return pl.pallas_call(
        functools.partial(merge_kernel, items_owned, per),
        out_shape=(piece(jnp.float32),) + (piece(jnp.bfloat16),) * (members - 1),
        in_specs=[SMEM, SMEM, SMEM, VMEM],
        out_specs=(VMEM,) * members,
        scratch_shapes=[pltpu.VMEM((items_owned, side, width), jnp.float32)],
        compiler_params=pltpu.CompilerParams(vmem_limit_bytes=12 << 20),
        name="merge",
    )(me, heard, slot, parts)


def body(
    tile_data,
    tile_user,
    tile_item,
    tile_word,
    tile_month,
    tile_live,
    user_need,
    item_need,
    user_slot,
    item_slot,
    user_factor,
    word_factor,
    month_factor,
):
    wide = lax.axis_size("wide")
    members = lax.axis_size("narrow")
    side = tile_data.shape[1]
    width = user_factor.shape[1]
    touched = item_need.shape[1]
    items_owned = item_slot.shape[0] // wide
    per_user = user_need.shape[1] // wide
    heard = lax.all_to_all(
        ask(user_need, item_need, wide), "wide", split_axis=0, concat_axis=0, tiled=True
    )
    me_wide = lax.axis_index("wide").reshape(1)
    plan, scale = rank(
        me_wide,
        per_user,
        tile_live,
        tile_user,
        tile_item,
        tile_word,
        tile_month,
        word_factor,
        month_factor,
        touched,
    )
    replies = answer(me_wide, heard, user_slot, user_factor.reshape(-1, side, width), per_user)
    fetched = list(replies)
    for d in reversed(range(1, wide)):
        fetched[d] = lax.ppermute(replies[d], "wide", [(k, k ^ d) for k in range(wide)])
    turned = turn(plan, tile_data, scale.shape[0])
    partial = contract(plan, scale, turned, fetched, touched)
    arrived = lax.all_to_all(
        partial.reshape(wide, -1, side, width), "wide", split_axis=0, concat_axis=0, tiled=True
    ).reshape(-1, side, width)
    me = lax.axis_index("narrow").reshape(1)
    pieces = merge(me, heard, item_slot, arrived, items_owned, members, touched // wide)
    rows = pieces[0]
    for d in range(1, members):
        got = lax.ppermute(pieces[d], "narrow", [(n, n ^ d) for n in range(members)])
        rows = rows + got.astype(jnp.float32)
    return rows.reshape(-1, width)


def solution(mesh):
    return jax.shard_map(
        body,
        mesh=mesh,
        in_specs=(
            P(("wide", "narrow"), None, None),
            P(("wide", "narrow")),
            P(("wide", "narrow")),
            P(("wide", "narrow")),
            P(("wide", "narrow")),
            P(("wide", "narrow")),
            P(("wide", "narrow"), None),
            P(("wide", "narrow"), None),
            P(),
            P(),
            P("wide", None),
            P(),
            P(),
        ),
        out_specs=P(("wide", "narrow"), None),
        check_vma=False,
    )
```

time: 188 us -> 71 us (0.38)
  other arithmetic: 46.9 us -> 0.76 us
  local copies, waits for them, and re-layouts: 43.6 us -> 6.36 us
  waiting for transfers between devices: 47.2 us -> 20.3 us
  Pallas kernels: 0 us -> 18.8 us
  matrix products: 13.8 us -> 0 us
  between operations: 14.1 us -> 0.77 us
  starting transfers between devices: 20.5 us -> 23.6 us
    scatter-add x1 -> x0, other arithmetic: 41.9 us -> none  [shards(): jax.ops.segment_sum(contrib, group_ids, num_segments=touched + 1)[:touched]]
    reduce_scatter x1 -> x0, waiting for transfers between devices: 24.1 us -> none  [shards(): lax.psum_scatter(owner_sum, 'narrow', scatter_dimension=0, tiled=True)]
    dot_general x2 -> x0, local copies, waits for them, and re-layouts: 22.4 us -> none  [the longest x1 21.1 us: shards(): jnp.einsum('tab,tar->tbr', tile_data, scaled, preferred_element_type=jnp....]
    gather x7 -> x0, local copies, waits for them, and re-layouts: 19.4 us -> none  [the longest x1 10.7 us: shards(): fetched[tile_user].astype(jnp.float32) * word_month[:, None, :]]
    pallas_call x0 -> x6, Pallas kernels: none -> 18.8 us  [the longest x1 6.27 us: rank(): pl.pallas_call(functools.partial(rank_kernel, per, pads), out_shape=(shap...]
    dot_general x2 -> x0, matrix products: 13.8 us -> none  [the longest x1 12.9 us: shards(): jnp.einsum('tab,tar->tbr', tile_data, scaled, preferred_element_type=jnp....]
    ppermute x0 -> x10, starting transfers between devices: none -> 12.9 us  [the longest x7 11 us: body(): lax.ppermute(replies[d], 'wide', [(k, k ^ d) for k in range(wide)])]
    all_to_all x4 -> x2, starting transfers between devices: 20.4 us -> 10.7 us  [the longest x1 7.29 us: body(): lax.all_to_all(ask(user_need, item_need, wide), 'wide', split_axis=0, con...]
  transfers between devices with their start and end apart: 5 -> 12, of which waited for: 4 -> 4; matrix products, arithmetic and copies ran while one was open for 52% -> 0% of each run, Pallas kernels for 0% -> 15%
where the time goes in v1:
time: 71 us; the launch traced here: 70.6 us
  starting transfers between devices  23.6 us (33%)
  waiting for transfers between devices  20.3 us (29%)
  Pallas kernels  18.8 us (26%)
  local copies, waits for them, and re-layouts  6.36 us (9%)
  between operations  0.77 us (1%)
  other arithmetic  0.76 us (1%)
    ppermute x7, starting transfers between devices, body(): lax.ppermute(replies[d], 'wide', [(k, k ^ d) for k in range(wide)])  11 us
    all_to_all x1, waiting for transfers between devices, body(): lax.all_to_all(partial.reshape(wide, -1, side, width), 'wide', split_axis...  8.15 us
    all_to_all x1, starting transfers between devices, body(): lax.all_to_all(ask(user_need, item_need, wide), 'wide', split_axis=0, con...  7.29 us
    unnamed x12, local copies, waits for them, and re-layouts  6.36 us
    ppermute x3, waiting for transfers between devices, body(): lax.ppermute(pieces[d], 'narrow', [(n, n ^ d) for n in range(members)])  6.32 us
    pallas_call x1, Pallas kernels, rank(): pl.pallas_call(functools.partial(rank_kernel, per, pads), out_shape=(shap...  6.27 us
    all_to_all x1, waiting for transfers between devices, body(): lax.all_to_all(ask(user_need, item_need, wide), 'wide', split_axis=0, con...  5.77 us
    pallas_call x1, Pallas kernels, contract(): pl.pallas_call(contract_kernel, out_shape=jax.ShapeDtypeStruct((touched,...  5.45 us
  transfers between devices with their start and end apart: 12, of which 4 were waited for; matrix products, arithmetic and copies ran while one was open for 0% of the time, Pallas kernels for 15%

profile of v1, /device:TPU:0, one launch (start us, length us, event | category | flops | bytes accessed | tf_op | source)
XLA Modules:
  0.0 70.6 jit_solution(4506764749251116189)
XLA Ops:
  0.0 1.3 %ask.1 = s32[8,1,3]{2,1,0:T(1,128)} custom-call(s32[1,16]{1,0:T(1,128)} %user_need.1, s32[1,8]{1,0:T(1,128)} %item_need.1), custom_call_target="tpu_custom_call" | custom-call | tf_op jit(solution)/shard_map/ask/pallas_call | solution.py:224
  1.3 7.3 %all-to-all-start = ((s32[8,1,3]{2,1,0:T(1,128)}), s32[8,1,3]{2,1,0:T(1,128)S(1)}, u32[]{:S(2)}, u32[]{:S(2)}) async-start(s32[8,1,3]{2,1,0:T(1,128)} %ask.1), calls=%async_computation | async-start | bytes 8192 | tf_op jit(solution)/shard_map/all_to_all | solution.py:365
  9.2 5.8 %all-to-all-done.heard = s32[8,1,3]{2,1,0:T(1,128)S(1)} async-done(((s32[8,1,3]{2,1,0:T(1,128)}), s32[8,1,3]{2,1,0:T(1,128)S(1)}, u32[]{:S(2)}, u32[]{:S(2)}) %all-to-all-start) | async-done | bytes 128 | tf_op jit(solution)/shard_map/all_to_all | solution.py:365
  15.0 0.0 copy-start.4
  15.0 1.0 %copy-done.4 = bf16[2048,128]{1,0:T(8,128)(2,1)S(1)} copy-done((bf16[2048,128]{1,0:T(8,128)(2,1)S(1)}, bf16[2048,128]{1,0:T(8,128)(2,1)}, u32[]{:S(2)}) %copy-start.4) | copy-done | bytes 524312
  16.0 0.0 copy-start.5
  16.1 0.7 copy-done.5
  16.7 0.7 answer.1
  17.4 0.6 collective-permute-start
  18.0 0.6 collective-permute-start.1
  18.6 6.3 %rank.1 = (s32[949]{0:T(1024)}, f32[448,128]{1,0:T(8,128)}) custom-call(s32[1]{0:T(128)} %bitcast.1.me, s32[1]{0:T(128)S(6)} %copy.15.live, s32[320]{0:T(512)} %user.1, s32[320]{0:T(512)} %word.1, s32[320]{0:T(512)} %month.1, s32[320]{0:T(512)} %item.1, bf16[4096,128]{1,0:T(8,128)(2,1)} %words.1, bf16[1000,128]{1,0:T(8,128)(2,1)} %months.1), custom_call_target="tpu_custom_call" | custom-call | flops 8589934592 | bytes 33554432 | tf_op jit(solution)/shard_map/rank/pallas_call | solution.py:148
  24.8 2.2 %collective-permute-start.2 = (bf16[2,128,128]{2,1,0:T(8,128)(2,1)S(1)}, bf16[2,128,128]{2,1,0:T(8,128)(2,1)S(1)}, u32[]{:S(2)}, u32[]{:S(2)}) collective-permute-start(bf16[2,128,128]{2,1,0:T(8,128)(2,1)S(1)} %get-tuple-element.24), channel_id=1, source_target_pairs={{0,12},{4,8},{8,4},{12,0},{16,28},{20,24},{24,20},{28,16},{1,13},{... | collective-permute-start | bytes 196616 | tf_op jit(solution)/shard_map/ppermute | solution.py:384
  27.0 0.5 collective-permute-start.3
  27.5 2.7 %collective-permute-start.4 = (bf16[2,128,128]{2,1,0:T(8,128)(2,1)S(1)}, bf16[2,128,128]{2,1,0:T(8,128)(2,1)S(1)}, u32[]{:S(2)}, u32[]{:S(2)}) collective-permute-start(bf16[2,128,128]{2,1,0:T(8,128)(2,1)S(1)} %get-tuple-element.26), channel_id=1, source_target_pairs={{0,20},{4,16},{8,28},{12,24},{16,4},{20,0},{24,12},{28,8},{1,21},{... | collective-permute-start | bytes 196616 | tf_op jit(solution)/shard_map/ppermute | solution.py:384
  30.2 0.0 collective-permute-done.refs_1_
  30.2 0.3 collective-permute-start.5
  30.5 0.0 collective-permute-done.1.refs_2_
  30.5 4.2 %collective-permute-start.6 = (bf16[2,128,128]{2,1,0:T(8,128)(2,1)S(1)}, bf16[2,128,128]{2,1,0:T(8,128)(2,1)S(1)}, u32[]{:S(2)}, u32[]{:S(2)}) collective-permute-start(bf16[2,128,128]{2,1,0:T(8,128)(2,1)S(1)} %get-tuple-element.28), channel_id=1, source_target_pairs={{0,28},{4,24},{8,20},{12,16},{16,12},{20,8},{24,4},{28,0},{1,29},{... | collective-permute-start | bytes 196616 | tf_op jit(solution)/shard_map/ppermute | solution.py:384
  34.7 0.0 copy-start
  34.7 4.0 %copy-done = bf16[320,128,128]{2,1,0:T(8,128)(2,1)S(1)} copy-done((bf16[320,128,128]{2,1,0:T(8,128)(2,1)S(1)}, bf16[320,128,128]{2,1,0:T(8,128)(2,1)}, u32[]{:S(2)}) %copy-start) | copy-done | bytes 10485784
  38.7 0.0 copy-start.2
  38.7 0.7 copy-done.2
  39.3 0.0 copy-start.1
  39.3 0.0 copy-start.3
  39.3 4.3 %turn.1.turned = bf16[448,128,128]{2,1,0:T(8,128)(2,1)S(1)} custom-call(s32[949]{0:T(1024)S(1)} %copy-done.2, bf16[320,128,128]{2,1,0:T(8,128)(2,1)S(1)} %copy-done), custom_call_target="tpu_custom_call" | custom-call | flops 1073741824 | bytes 20971520 | tf_op jit(solution)/shard_map/turn/pallas_call | solution.py:199
  43.6 0.0 collective-permute-done.2.refs_3_
  43.6 0.0 collective-permute-done.3.refs_4_
  43.6 0.0 collective-permute-done.4.refs_5_
  43.6 0.0 collective-permute-done.5.refs_6_
  43.6 0.0 collective-permute-done.6.refs_7_
  43.7 0.0 copy-done.1
  43.7 5.4 %contract.1 = bf16[8,128,128]{2,1,0:T(8,128)(2,1)} custom-call(s32[949]{0:T(1024)S(1)} %copy-done.2, f32[448,128]{1,0:T(8,128)S(1)} %copy-done.1, bf16[448,128,128]{2,1,0:T(8,128)(2,1)S(1)} %turn.1.turned, bf16[2,128,128]{2,1,0:T(8,128)(2,1)S(1)} %get-tuple-element.21.refs_0_, bf16[2,128,128]{2,1,0:T(8,128)(2,1)S(1)} %collective-permute-done.refs_1_, ...), custom_call_target="tpu_custom_call" | custom-call | flops 1879048192 | bytes 7340032 | tf_op jit(solution)/shard_map/contract/pallas_call | solution.py:288
  49.1 3.4 %all-to-all-start.1 = ((bf16[8,1,128,128]{3,2,1,0:T(8,128)(2,1)}), bf16[8,1,128,128]{3,2,1,0:T(8,128)(2,1)S(1)}, u32[]{:S(2)}, u32[]{:S(2)}) async-start(bf16[8,1,128,128]{3,2,1,0:T(8,128)(2,1)} %bitcast.4), calls=%async_computation.1 | async-start | bytes 524288 | tf_op jit(solution)/shard_map/all_to_all | solution.py:387
  52.5 8.2 %all-to-all-done.1 = bf16[8,1,128,128]{3,2,1,0:T(8,128)(2,1)S(1)} async-done(((bf16[8,1,128,128]{3,2,1,0:T(8,128)(2,1)}), bf16[8,1,128,128]{3,2,1,0:T(8,128)(2,1)S(1)}, u32[]{:S(2)}, u32[]{:S(2)}) %all-to-all-start.1) | async-done | bytes 262176 | tf_op jit(solution)/shard_map/all_to_all | solution.py:387
  60.7 0.0 copy-done.3
  60.7 0.9 %merge.1 = (f32[4,128,128]{2,1,0:T(8,128)S(1)}, bf16[4,128,128]{2,1,0:T(8,128)(2,1)S(1)}, bf16[4,128,128]{2,1,0:T(8,128)(2,1)S(1)}, bf16[4,128,128]{2,1,0:T(8,128)(2,1)S(1)}) custom-call(s32[1]{0:T(128)} %bitcast.me, s32[8,1,3]{2,1,0:T(1,128)S(1)} %all-to-all-done.heard, s32[128]{0:T(128)S(1)} %copy-done.3, bf16[8,128,128]{2,1,0:T(8,128)(2,1)S(1)} %bitcast.8), custom_call_target="tpu_custom_call" | custom-call | tf_op jit(solution)/shard_map/merge/pallas_call | solution.py:332
  61.6 0.1 collective-permute-start.7
  61.6 0.5 collective-permute-start.8
  62.1 1.4 %collective-permute-start.9 = (bf16[4,128,128]{2,1,0:T(8,128)(2,1)S(1)}, bf16[4,128,128]{2,1,0:T(8,128)(2,1)S(1)}, u32[]{:S(2)}, u32[]{:S(2)}) collective-permute-start(bf16[4,128,128]{2,1,0:T(8,128)(2,1)S(1)} %get-tuple-element.32), channel_id=1, source_target_pairs={{0,3},{1,2},{2,1},{3,0},{4,7},{5,6},{6,5},{7,4},{8,11},{9,10},{10,... | collective-permute-start | bytes 393224 | tf_op jit(solution)/shard_map/ppermute | solution.py:394
  63.5 0.0 collective-permute-done.7
  63.5 4.6 %collective-permute-done.8 = bf16[4,128,128]{2,1,0:T(8,128)(2,1)S(1)} collective-permute-done((bf16[4,128,128]{2,1,0:T(8,128)(2,1)S(1)}, bf16[4,128,128]{2,1,0:T(8,128)(2,1)S(1)}, u32[]{:S(2)}, u32[]{:S(2)}) %collective-permute-start.8) | collective-permute-done | bytes 131104 | tf_op jit(solution)/shard_map/ppermute | solution.py:394
  68.1 1.7 %collective-permute-done.9 = bf16[4,128,128]{2,1,0:T(8,128)(2,1)S(1)} collective-permute-done((bf16[4,128,128]{2,1,0:T(8,128)(2,1)S(1)}, bf16[4,128,128]{2,1,0:T(8,128)(2,1)S(1)}, u32[]{:S(2)}, u32[]{:S(2)}) %collective-permute-start.9) | collective-permute-done | bytes 131104 | tf_op jit(solution)/shard_map/ppermute | solution.py:394
  69.8 0.8 %convert_add_fusion = f32[4,128,128]{2,1,0:T(8,128)} fusion(bf16[4,128,128]{2,1,0:T(8,128)(2,1)S(1)} %collective-permute-done.9, bf16[4,128,128]{2,1,0:T(8,128)(2,1)S(1)} %collective-permute-done.8, f32[4,128,128]{2,1,0:T(8,128)S(1)} %get-tuple-element.29, bf16[4,128,128]{2,1,0:T(8,128)(2,1)S(1)} %collective-permute-done.7), kind=kLoop, calls=%fused_computation | loop fusion | flops 393216 | bytes 917504 | tf_op jit(solution)/shard_map/add | solution.py:395
Async XLA Ops:
  1.3 13.7 %all-to-all-start = ((s32[8,1,3]{2,1,0:T(1,128)}), s32[8,1,3]{2,1,0:T(1,128)S(1)}, u32[]{:S(2)}, u32[]{:S(2)}) async-start(s32[8,1,3]{2,1,0:T(1,128)} %ask.1), calls=%async_computation | async-start | bytes 8192 | tf_op jit(solution)/shard_map/all_to_all | solution.py:365
  15.0 1.0 %copy-start.4 = (bf16[2048,128]{1,0:T(8,128)(2,1)S(1)}, bf16[2048,128]{1,0:T(8,128)(2,1)}, u32[]{:S(2)}) copy-start(bf16[2048,128]{1,0:T(8,128)(2,1)} %param.23) | copy-start | bytes 1572868
  16.0 0.7 copy-start.5
  17.4 12.9 %collective-permute-start = (bf16[2,128,128]{2,1,0:T(8,128)(2,1)S(1)}, bf16[2,128,128]{2,1,0:T(8,128)(2,1)S(1)}, u32[]{:S(2)}, u32[]{:S(2)}) collective-permute-start(bf16[2,128,128]{2,1,0:T(8,128)(2,1)S(1)} %get-tuple-element.22), channel_id=1, source_target_pairs={{0,4},{4,0},{8,12},{12,8},{16,20},{20,16},{24,28},{28,24},{1,5},{5... | collective-permute-start | bytes 196616 | tf_op jit(solution)/shard_map/ppermute | solution.py:384
  18.0 12.5 %collective-permute-start.1 = (bf16[2,128,128]{2,1,0:T(8,128)(2,1)S(1)}, bf16[2,128,128]{2,1,0:T(8,128)(2,1)S(1)}, u32[]{:S(2)}, u32[]{:S(2)}) collective-permute-start(bf16[2,128,128]{2,1,0:T(8,128)(2,1)S(1)} %get-tuple-element.23), channel_id=1, source_target_pairs={{0,8},{4,12},{8,0},{12,4},{16,24},{20,28},{24,16},{28,20},{1,9},{5... | collective-permute-start | bytes 196616 | tf_op jit(solution)/shard_map/ppermute | solution.py:384
  24.8 18.8 %collective-permute-start.2 = (bf16[2,128,128]{2,1,0:T(8,128)(2,1)S(1)}, bf16[2,128,128]{2,1,0:T(8,128)(2,1)S(1)}, u32[]{:S(2)}, u32[]{:S(2)}) collective-permute-start(bf16[2,128,128]{2,1,0:T(8,128)(2,1)S(1)} %get-tuple-element.24), channel_id=1, source_target_pairs={{0,12},{4,8},{8,4},{12,0},{16,28},{20,24},{24,20},{28,16},{1,13},{... | collective-permute-start | bytes 196616 | tf_op jit(solution)/shard_map/ppermute | solution.py:384
  27.0 16.6 %collective-permute-start.3 = (bf16[2,128,128]{2,1,0:T(8,128)(2,1)S(1)}, bf16[2,128,128]{2,1,0:T(8,128)(2,1)S(1)}, u32[]{:S(2)}, u32[]{:S(2)}) collective-permute-start(bf16[2,128,128]{2,1,0:T(8,128)(2,1)S(1)} %get-tuple-element.25), channel_id=1, source_target_pairs={{0,16},{4,20},{8,24},{12,28},{16,0},{20,4},{24,8},{28,12},{1,17},{... | collective-permute-start | bytes 196616 | tf_op jit(solution)/shard_map/ppermute | solution.py:384
  27.5 16.1 %collective-permute-start.4 = (bf16[2,128,128]{2,1,0:T(8,128)(2,1)S(1)}, bf16[2,128,128]{2,1,0:T(8,128)(2,1)S(1)}, u32[]{:S(2)}, u32[]{:S(2)}) collective-permute-start(bf16[2,128,128]{2,1,0:T(8,128)(2,1)S(1)} %get-tuple-element.26), channel_id=1, source_target_pairs={{0,20},{4,16},{8,28},{12,24},{16,4},{20,0},{24,12},{28,8},{1,21},{... | collective-permute-start | bytes 196616 | tf_op jit(solution)/shard_map/ppermute | solution.py:384
  30.2 13.4 %collective-permute-start.5 = (bf16[2,128,128]{2,1,0:T(8,128)(2,1)S(1)}, bf16[2,128,128]{2,1,0:T(8,128)(2,1)S(1)}, u32[]{:S(2)}, u32[]{:S(2)}) collective-permute-start(bf16[2,128,128]{2,1,0:T(8,128)(2,1)S(1)} %get-tuple-element.27), channel_id=1, source_target_pairs={{0,24},{4,28},{8,16},{12,20},{16,8},{20,12},{24,0},{28,4},{1,25},{... | collective-permute-start | bytes 196616 | tf_op jit(solution)/shard_map/ppermute | solution.py:384
  30.5 13.1 %collective-permute-start.6 = (bf16[2,128,128]{2,1,0:T(8,128)(2,1)S(1)}, bf16[2,128,128]{2,1,0:T(8,128)(2,1)S(1)}, u32[]{:S(2)}, u32[]{:S(2)}) collective-permute-start(bf16[2,128,128]{2,1,0:T(8,128)(2,1)S(1)} %get-tuple-element.28), channel_id=1, source_target_pairs={{0,28},{4,24},{8,20},{12,16},{16,12},{20,8},{24,4},{28,0},{1,29},{... | collective-permute-start | bytes 196616 | tf_op jit(solution)/shard_map/ppermute | solution.py:384
  34.7 4.0 %copy-start = (bf16[320,128,128]{2,1,0:T(8,128)(2,1)S(1)}, bf16[320,128,128]{2,1,0:T(8,128)(2,1)}, u32[]{:S(2)}) copy-start(bf16[320,128,128]{2,1,0:T(8,128)(2,1)} %tiles.1) | copy-start | bytes 31457284
  38.7 0.7 copy-start.2
  39.3 4.3 %copy-start.1 = (f32[448,128]{1,0:T(8,128)S(1)}, f32[448,128]{1,0:T(8,128)}, u32[]{:S(2)}) copy-start(f32[448,128]{1,0:T(8,128)} %get-tuple-element.20.scale) | copy-start | bytes 688132
  39.3 21.4 %copy-start.3 = (s32[128]{0:T(128)S(1)}, s32[128]{0:T(128)}, u32[]{:S(2)}) copy-start(s32[128]{0:T(128)} %slot.3) | copy-start | bytes 1540
  49.1 11.6 %all-to-all-start.1 = ((bf16[8,1,128,128]{3,2,1,0:T(8,128)(2,1)}), bf16[8,1,128,128]{3,2,1,0:T(8,128)(2,1)S(1)}, u32[]{:S(2)}, u32[]{:S(2)}) async-start(bf16[8,1,128,128]{3,2,1,0:T(8,128)(2,1)} %bitcast.4), calls=%async_computation.1 | async-start | bytes 524288 | tf_op jit(solution)/shard_map/all_to_all | solution.py:387
  61.6 1.9 %collective-permute-start.7 = (bf16[4,128,128]{2,1,0:T(8,128)(2,1)S(1)}, bf16[4,128,128]{2,1,0:T(8,128)(2,1)S(1)}, u32[]{:S(2)}, u32[]{:S(2)}) collective-permute-start(bf16[4,128,128]{2,1,0:T(8,128)(2,1)S(1)} %get-tuple-element.30), channel_id=1, source_target_pairs={{0,1},{1,0},{2,3},{3,2},{4,5},{5,4},{6,7},{7,6},{8,9},{9,8},{10,11... | collective-permute-start | bytes 393224 | tf_op jit(solution)/shard_map/ppermute | solution.py:394
  61.6 6.4 %collective-permute-start.8 = (bf16[4,128,128]{2,1,0:T(8,128)(2,1)S(1)}, bf16[4,128,128]{2,1,0:T(8,128)(2,1)S(1)}, u32[]{:S(2)}, u32[]{:S(2)}) collective-permute-start(bf16[4,128,128]{2,1,0:T(8,128)(2,1)S(1)} %get-tuple-element.31), channel_id=1, source_target_pairs={{0,2},{1,3},{2,0},{3,1},{4,6},{5,7},{6,4},{7,5},{8,10},{9,11},{10,... | collective-permute-start | bytes 393224 | tf_op jit(solution)/shard_map/ppermute | solution.py:394
  62.1 7.7 %collective-permute-start.9 = (bf16[4,128,128]{2,1,0:T(8,128)(2,1)S(1)}, bf16[4,128,128]{2,1,0:T(8,128)(2,1)S(1)}, u32[]{:S(2)}, u32[]{:S(2)}) collective-permute-start(bf16[4,128,128]{2,1,0:T(8,128)(2,1)S(1)} %get-tuple-element.32), channel_id=1, source_target_pairs={{0,3},{1,2},{2,1},{3,0},{4,7},{5,6},{6,5},{7,4},{8,11},{9,10},{10,... | collective-permute-start | bytes 393224 | tf_op jit(solution)/shard_map/ppermute | solution.py:394
